TPU v7x, 256 devices: a whole 4x4x8 slice. The times are simulated.
256 devices in a mesh: dp: 64 (over z, x, core), head: 4 (over y).
Axes of the slice: x: 4, y: 4, z: 8, core: 2. Of those that a mesh axis runs over, the one named last changes fastest.
Arguments:
- queries: bfloat16 [32768, 2048], P('dp', 'head'), may hold values from -48 to 48
- encodings: bfloat16 [1024, 128, 896], P('dp', None, 'head'), may hold values from -12 to 12
- neighbour_ids: int32 [512, 2], P('dp'), may hold values from 0 to 1023, as said below
- block_place: int32 [1024], replicated, may hold values from 0 to 1023, as said below
- query_weight: bfloat16 [4096, 2048], P(None, 'head'), may hold values from -1 to 1
- key_weight: bfloat16 [896, 2048], P(None, 'head'), may hold values from -1 to 1
- value_weight: bfloat16 [896, 2048], P(None, 'head'), may hold values from -0.1875 to 0.1875
- attn_grad: bfloat16 [32768, 2048], P('dp', 'head'), may hold values from -24 to 24
Outputs:
- query_input_grad: bfloat16 [32768, 4096], P('dp', 'head')
- encodings_grad: bfloat16 [1024, 128, 896], P('dp', None, 'head')
- key_weight_grad: float32 [896, 2048], P('dp', 'head')
- value_weight_grad: float32 [896, 2048], P('dp', 'head')
Inputs may be any that keep to these rules, and one draw needn't show every extreme that they name: `neighbour_ids`: block b is stored at position block_place[b] of encodings, on the index block_place[b] // 16 of dp. Of the 16 slots of the spans of one index of dp, each index of dp stores the blocks of 1 or 0, and some index stores those of exactly 1. `block_place`: A permutation: every position once.
All inputs are finite; a program needn't handle non-finite values.
Results may differ from a plain program's by a relative error of at most 0.012.
The roundings to bfloat16 on the way count: a program that leaves them out, or rounds other values in their place, can miss the bound.
Values may be sent and summed in bfloat16 or wider, within the bound.
No kernel may reach another device: no remote copies, remote signals or barrier semaphores. Data moves between devices by JAX's collectives and lax.ppermute only.
A program may use at most 128 MiB of HBM per device.

v0:
```python
import math

import jax
import jax.numpy as jnp
from jax import lax
from jax.sharding import PartitionSpec as P

DH = 128
E = 896
CH = 64
NTOK = 128
NEIGH = 2


def shards(
    queries,
    encodings,
    neighbour_ids,
    block_place,
    query_weight,
    key_weight,
    value_weight,
    attn_grad,
):
    dp_count = lax.axis_size("dp")
    own_blocks = encodings.shape[0]
    span_count = neighbour_ids.shape[0]
    block_names = neighbour_ids.reshape(-1)
    slot_count = block_names.shape[0]
    capacity = -(-slot_count // dp_count)
    position = block_place[block_names]
    owner_dev = position // own_blocks
    local_slot = position % own_blocks
    slot_order = jnp.arange(slot_count, dtype=jnp.int32)
    same_owner = (owner_dev[:, None] == owner_dev[None, :]) & (
        slot_order[None, :] < slot_order[:, None]
    )
    slot_rank = jnp.sum(same_owner.astype(jnp.int32), axis=1)
    device_match = owner_dev[:, None, None] == jnp.arange(dp_count, dtype=jnp.int32)[None, :, None]
    rank_match = slot_rank[:, None, None] == jnp.arange(capacity, dtype=jnp.int32)[None, None, :]
    requests = (
        jnp.sum(jnp.where(device_match & rank_match, local_slot[:, None, None] + 1, 0), axis=0) - 1
    )
    asked_rows = lax.all_to_all(requests, "dp", split_axis=0, concat_axis=0, tiled=True)
    valid_mask = asked_rows >= 0
    local_index = jnp.maximum(asked_rows, 0)
    blank = jnp.zeros((), jnp.bfloat16)
    whole_own = lax.all_gather(encodings, "head", axis=2, tiled=True)
    packed = jnp.where(valid_mask[:, :, None, None], whole_own[local_index], blank)
    received = lax.all_to_all(packed, "dp", split_axis=0, concat_axis=0, tiled=True)
    slot_blocks = received[owner_dev, slot_rank]
    flat_rows = slot_blocks.reshape(-1, E)
    both_weights = jnp.concatenate([key_weight, value_weight], axis=1)
    head_cols = key_weight.shape[1]
    local_heads = head_cols // DH
    projected = jnp.dot(flat_rows, both_weights, preferred_element_type=jnp.float32).astype(
        jnp.bfloat16
    )
    key_rows = projected[:, :head_cols].reshape(span_count, NEIGH * NTOK, local_heads, DH)
    value_rows = projected[:, head_cols:].reshape(span_count, NEIGH * NTOK, local_heads, DH)
    query_heads = queries.reshape(span_count, CH, local_heads, DH)
    grad_heads = attn_grad.reshape(span_count, CH, local_heads, DH)
    score_scale = 1.0 / math.sqrt(DH)
    scores = (
        jnp.einsum("cqhd,ckhd->chqk", query_heads, key_rows, preferred_element_type=jnp.float32)
        * score_scale
    )
    shifted = jnp.exp(scores - jnp.max(scores, axis=-1, keepdims=True))
    prob_rows = shifted / jnp.sum(shifted, axis=-1, keepdims=True)
    prob_half = prob_rows.astype(jnp.bfloat16)
    grad_probs = jnp.einsum(
        "cqhd,ckhd->chqk", grad_heads, value_rows, preferred_element_type=jnp.float32
    )
    row_delta = jnp.sum(prob_rows * grad_probs, axis=-1, keepdims=True)
    grad_scores = (prob_rows * (grad_probs - row_delta) * score_scale).astype(jnp.bfloat16)
    value_grad = jnp.einsum(
        "chqk,cqhd->ckhd", prob_half, grad_heads, preferred_element_type=jnp.float32
    ).astype(jnp.bfloat16)
    key_grad = jnp.einsum(
        "chqk,cqhd->ckhd", grad_scores, query_heads, preferred_element_type=jnp.float32
    ).astype(jnp.bfloat16)
    query_grad = jnp.einsum(
        "chqk,ckhd->cqhd", grad_scores, key_rows, preferred_element_type=jnp.float32
    ).astype(jnp.bfloat16)
    partial_input = jnp.dot(
        query_grad.reshape(-1, head_cols), query_weight.T, preferred_element_type=jnp.float32
    )
    query_input_grad = lax.psum_scatter(
        partial_input.astype(jnp.bfloat16), "head", scatter_dimension=1, tiled=True
    )
    both_grads = jnp.concatenate(
        [key_grad.reshape(-1, head_cols), value_grad.reshape(-1, head_cols)], axis=1
    )
    weight_grads = lax.psum_scatter(
        lax.dot_general(
            flat_rows, both_grads, (((0,), (0,)), ((), ())), preferred_element_type=jnp.float32
        ),
        "dp",
        scatter_dimension=0,
        tiled=True,
    )
    slot_partial = jnp.dot(both_grads, both_weights.T, preferred_element_type=jnp.float32).reshape(
        slot_count, NTOK, E
    )
    slot_grad = lax.psum_scatter(
        slot_partial.astype(jnp.bfloat16), "head", scatter_dimension=2, tiled=True
    )
    quarter = slot_grad.shape[2]
    outgoing = (
        jnp.zeros((dp_count, capacity, NTOK, quarter), jnp.bfloat16)
        .at[owner_dev, slot_rank]
        .set(slot_grad)
    )
    returned = lax.all_to_all(outgoing, "dp", split_axis=0, concat_axis=0, tiled=True)
    block_match = (
        local_index.reshape(-1)[None, :] == jnp.arange(own_blocks, dtype=jnp.int32)[:, None]
    )
    target = (block_match & valid_mask.reshape(-1)[None, :]).astype(jnp.bfloat16)
    encodings_grad = jnp.dot(
        target, returned.reshape(dp_count * capacity, -1), preferred_element_type=jnp.float32
    )
    encodings_grad = encodings_grad.reshape(own_blocks, NTOK, quarter).astype(jnp.bfloat16)
    return (
        query_input_grad,
        encodings_grad,
        weight_grads[:, :head_cols],
        weight_grads[:, head_cols:],
    )


def solution(mesh):
    in_specs = (
        P("dp", "head"),
        P("dp", None, "head"),
        P("dp", None),
        P(),
        P(None, "head"),
        P(None, "head"),
        P(None, "head"),
        P("dp", "head"),
    )
    out_specs = (P("dp", "head"), P("dp", None, "head"), P("dp", "head"), P("dp", "head"))
    return jax.shard_map(shards, mesh=mesh, in_specs=in_specs, out_specs=out_specs, check_vma=False)
```

profile of v0, /device:TPU:1, one launch (start us, length us, event | category | flops | bytes accessed | tf_op | source)
XLA Modules:
  0.0 862.3 jit_solution(8906431637875091830)
XLA Ops:
  7.2 2.5 copy.111
  11.0 22.2 %all_to_all.16 = s32[64,1,1]{2,1,0:T(1,128)S(1)} all-to-all(s32[64,1,1]{2,1,0:T(1,128)S(1)} %copy.110), channel_id=1, replica_groups=mesh['dp'=64,'head'=4] {'dp'}, dimensions={0} | all-to-all | bytes 512 | tf_op jit(solution)/shard_map/all_to_all | solution.py:44
  35.6 24.8 %all-gather.2.cloned.1.call-done = bf16[16,128,896]{1,0,2:T(8,128)(2,1)} async-done(((bf16[16,128,224]{1,0,2:T(8,128)(2,1)}), bf16[16,128,896]{1,0,2:T(8,128)(2,1)}) %all-gather.2.cloned.1.call-update) | async-done | bytes 3670032 | tf_op jit(solution)/shard_map/all_gather | solution.py:48
  60.5 6.5 copy.112
  66.9 10.0 %gather_fusion.1 = bf16[64,128,896]{2,1,0:T(8,128)(2,1)} fusion(bf16[16,128,896]{2,1,0:T(8,128)(2,1)} %copy.112, s32[1024]{0:T(1024)S(1)} %pad_clamp_fusion), kind=kCustom, calls=%fused_computation.1 | custom fusion | bytes 29360384 | tf_op jit(solution)/shard_map/gather | solution.py:49
  77.0 13.5 %fusion.2 = bf16[64,1,128,896]{3,2,1,0:T(8,128)(2,1)} fusion(bf16[64,128,896]{2,1,0:T(8,128)(2,1)} %gather_fusion.1, pred[64]{0:T(512)(128)(4,1)S(1)} %compare_reduce_fusion), kind=kLoop, calls=%fused_computation.7 | loop fusion | flops 7340032 | bytes 29360192 | tf_op jit(solution)/shard_map/jit(_where)/select_n | solution.py:49
  90.5 11.1 %all-to-all-start.1 = ((bf16[64,1,128,896]{3,2,1,0:T(8,128)(2,1)}), bf16[64,1,128,896]{3,2,1,0:T(8,128)(2,1)}, u32[]{:S(2)}, u32[]{:S(2)}) async-start(bf16[64,1,128,896]{3,2,1,0:T(8,128)(2,1)} %fusion.2), calls=%async_computation.1 | async-start | bytes 29360128 | tf_op jit(solution)/shard_map/all_to_all | solution.py:50
  104.6 317.0 %all-to-all-done.1 = bf16[64,1,128,896]{3,2,1,0:T(8,128)(2,1)} async-done(((bf16[64,1,128,896]{3,2,1,0:T(8,128)(2,1)}), bf16[64,1,128,896]{3,2,1,0:T(8,128)(2,1)}, u32[]{:S(2)}, u32[]{:S(2)}) %all-to-all-start.1) | async-done | bytes 14680096 | tf_op jit(solution)/shard_map/all_to_all | solution.py:50
  421.6 8.1 gather_fusion.2
  429.7 7.0 convolution_convert_fusion.1
  439.0 2.5 reshape.339
  444.6 4.0 reshape.341
  448.5 3.8 fusion.8
  452.3 7.9 convert_bitcast_fusion
  460.2 17.2 %convert_bitcast_fusion.1 = bf16[8,256,4,128]{3,1,2,0:T(8,128)(2,1)} fusion(f32[8,4,256,64]{2,3,1,0:T(8,128)} %fusion.8, bf16[8,64,4,128]{3,2,1,0:T(4,128)(2,1)S(1)} %reshape.340, f32[8,4,64,256]{3,2,1,0:T(8,128)} %get-tuple-element.41, f32[8,4,64]{2,1,0:T(4,128)S(1)} %get-tuple-element.40), kind=kOutput, calls=%fused_computation.23 | convolution fusion | flops 138938624 | bytes 6823936 | tf_op jit(solution)/shard_map/chqk,cqhd->ckhd/dot_general | solution.py:79
  477.4 4.5 copy.121
  485.6 4.5 copy.123
  494.5 18.7 %convolution_convert_fusion.2 = bf16[2048,896]{1,0:T(8,128)(2,1)} fusion(bf16[2048,1024]{0,1:T(8,128)(2,1)S(1)} %constant_dynamic-update-slice_fusion.2, bf16[896,1024]{1,0:T(8,128)(2,1)S(1)} %copy-done.11), kind=kOutput, calls=%fused_computation.10 | convolution fusion | flops 3759931392 | bytes 9699328 | tf_op jit(solution)/shard_map/dot_general | solution.py:102
  513.2 6.1 copy.124
  519.3 9.1 %fusion.54 = f32[896,1024]{1,0:T(8,128)} fusion(bf16[2048,896]{1,0:T(8,128)(2,1)} %bitcast.125, bf16[2048,1024]{0,1:T(8,128)(2,1)} %copy-done.5), kind=kOutput, calls=%fused_computation.90 | convolution fusion | flops 3758096384 | bytes 11534336 | tf_op jit(solution)/shard_map/dot_general | solution.py:95
  528.5 14.8 %fusion.20 = bf16[8,64,4,128]{3,1,2,0:T(8,128)(2,1)S(1)} fusion(bf16[8,256,4,128]{3,2,1,0:T(4,128)(2,1)S(1)} %reshape.339, f32[8,4,256,64]{2,3,1,0:T(8,128)} %fusion.8, f32[8,4,64,256]{3,2,1,0:T(8,128)} %get-tuple-element.41, f32[8,4,64]{2,1,0:T(4,128)S(1)} %get-tuple-element.40), kind=kOutput, calls=%fused_computation.31 | convolution fusion | flops 138152192 | bytes 6823936 | tf_op jit(solution)/shard_map/chqk,ckhd->cqhd/dot_general | solution.py:82
  543.7 6.5 convolution_convert_fusion
  550.3 15.2 %reduce-scatter.5.cloned.1.call-done = bf16[16,128,224]{1,2,0:T(8,128)(2,1)} async-done(((bf16[16,128,896]{1,2,0:T(8,128)(2,1)}), bf16[16,128,224]{1,2,0:T(8,128)(2,1)}) %reduce-scatter.5.cloned.1.call-update) | async-done | bytes 917520 | tf_op jit(solution)/shard_map/reduce_scatter | solution.py:105
  567.8 2.9 scatter_fusion
  570.7 11.0 %all-to-all-start.2 = ((bf16[64,1,128,224]{2,3,1,0:T(8,128)(2,1)}), bf16[64,1,128,224]{2,3,1,0:T(8,128)(2,1)}, u32[]{:S(2)}, u32[]{:S(2)}) async-start(bf16[64,1,128,224]{2,3,1,0:T(8,128)(2,1)} %bitcast.117), calls=%async_computation.4 | async-start | bytes 7340032 | tf_op jit(solution)/shard_map/all_to_all | solution.py:114
  583.0 219.7 %all-reduce.3.cloned.1.call-done = f32[896,1024]{1,0:T(8,128)} async-done(((f32[896,1024]{1,0:T(8,128)}), f32[896,1024]{1,0:T(8,128)}) %all-reduce.3.cloned.1.call-update) | async-done | bytes 3670032
  804.2 6.2 copy.126
  810.4 9.7 %reshape.346 = bf16[64,28672]{1,0:T(8,128)(2,1)} reshape(bf16[64,1,128,224]{3,2,0,1:T(8,128)(2,1)} %copy.126) | data formatting | bytes 7340032 | tf_op jit(solution)/shard_map/reshape | solution.py:120
  820.2 8.0 dot_general.46
  828.2 6.6 copy.127
  834.7 2.7 convolution_convert_fusion.3
  838.6 16.9 %reduce-scatter.3.cloned.1.call-done = bf16[512,1024]{1,0:T(8,128)(2,1)} async-done(((bf16[512,4096]{1,0:T(8,128)(2,1)}), bf16[512,1024]{1,0:T(8,128)(2,1)}) %reduce-scatter.3.cloned.1.call-update) | async-done | bytes 1048592 | tf_op jit(solution)/shard_map/reduce_scatter | solution.py:88
  (68 shorter events, 26.2 us)
Async XLA Ops:
  7.2 2.7 copy-start
  7.2 2.5 copy-start.12
  7.2 53.3 %all-gather.2.cloned.1.call-start = ((), (), s32[]{:S(2)}) async-start(), calls=%async_computation.5 | async-start | bytes 4587520 | tf_op jit(solution)/shard_map/all_gather | solution.py:48
  90.4 11.2 %copy-start.8 = (bf16[512,512]{1,0:T(8,128)(2,1)S(1)}, bf16[512,512]{1,0:T(8,128)(2,1)}, u32[]{:S(2)}) copy-start(bf16[512,512]{1,0:T(8,128)(2,1)} %param.8) | copy-start | bytes 1572868
  90.5 331.2 %all-to-all-start.1 = ((bf16[64,1,128,896]{3,2,1,0:T(8,128)(2,1)}), bf16[64,1,128,896]{3,2,1,0:T(8,128)(2,1)}, u32[]{:S(2)}, u32[]{:S(2)}) async-start(bf16[64,1,128,896]{3,2,1,0:T(8,128)(2,1)} %fusion.2), calls=%async_computation.1 | async-start | bytes 29360128 | tf_op jit(solution)/shard_map/all_to_all | solution.py:50
  101.6 1.5 copy-start.6
  101.6 1.6 copy-start.7
  101.6 463.9 %reduce-scatter.5.cloned.1.call-start = ((), (), s32[]{:S(2)}) async-start(), calls=%async_computation.7 | async-start | bytes 4587520 | tf_op jit(solution)/shard_map/reduce_scatter | solution.py:105
  103.3 1.3 copy-start.9
  421.6 8.1 copy-start.10
  442.4 2.2 copy-start.2
  490.2 2.8 copy-start.4
  493.0 1.5 copy-start.11
  494.5 18.7 %copy-start.5 = (bf16[2048,1024]{0,1:T(8,128)(2,1)}, bf16[2048,1024]{0,1:T(8,128)(2,1)S(1)}, u32[]{:S(2)}) copy-start(bf16[2048,1024]{0,1:T(8,128)(2,1)S(1)} %constant_dynamic-update-slice_fusion.2) | copy-start | bytes 12582916
  519.2 283.4 %all-reduce.3.cloned.1.call-start = ((), (), s32[]{:S(2)}) async-start(), calls=%async_computation.8 | async-start | bytes 7340032
  528.4 327.1 %reduce-scatter.3.cloned.1.call-start = ((), (), s32[]{:S(2)}) async-start(), calls=%async_computation.6 | async-start | bytes 5242880 | tf_op jit(solution)/shard_map/reduce_scatter | solution.py:88
  565.5 2.3 copy-start.3
  570.7 11.0 %copy-start.13 = (u32[256]{0:T(256)S(1)}, u32[256]{0:T(256)}, u32[]{:S(2)}) copy-start(u32[256]{0:T(256)} %constant.70) | copy-start | bytes 3076
  570.7 233.5 %all-to-all-start.2 = ((bf16[64,1,128,224]{2,3,1,0:T(8,128)(2,1)}), bf16[64,1,128,224]{2,3,1,0:T(8,128)(2,1)}, u32[]{:S(2)}, u32[]{:S(2)}) async-start(bf16[64,1,128,224]{2,3,1,0:T(8,128)(2,1)} %bitcast.117), calls=%async_computation.4 | async-start | bytes 7340032 | tf_op jit(solution)/shard_map/all_to_all | solution.py:114
  828.2 27.4 %copy-start.1 = (s32[1024]{0:T(1024)S(1)}, s32[1024]{0:T(1024)}, u32[]{:S(2)}) copy-start(s32[1024]{0:T(1024)} %param.11) | copy-start | bytes 12292
Sparse Core Ops, SparseCore 0:
  10.4 50.0 all-gather.1
  519.4 46.1 reduce-scatter.4
  569.0 233.6 all-reduce.2
  805.7 49.8 reduce-scatter.2
where the time goes:
time: 863 us; the launch traced here: 862 us
  waiting for transfers between devices  594 us (69%)
  local copies, waits for them, and re-layouts  102 us (12%)
  matrix products  88.5 us (10%)
  starting transfers between devices  22.3 us (3%)
  blocking collectives  22.2 us (3%)
  other arithmetic  18.5 us (2%)
  between operations  14.8 us (2%)
    all_to_all x1, waiting for transfers between devices, shards(): lax.all_to_all(packed, 'dp', split_axis=0, concat_axis=0, tiled=True)  317 us
    unnamed x5, waiting for transfers between devices  220 us
    all_gather x1, waiting for transfers between devices, shards(): whole_own = lax.all_gather(encodings, 'head', axis=2, tiled=True)  24.8 us
    all_to_all x1, blocking collectives, shards(): lax.all_to_all(requests, 'dp', split_axis=0, concat_axis=0, tiled=True)  22.2 us
    dot_general x1, matrix products, shards(): jnp.dot(both_grads, both_weights.T, preferred_element_type=jnp.float32)  18.7 us
  transfers between devices with their start and end apart: 6, of which 5 were waited for; matrix products, arithmetic and copies ran while one was open for 9% of the time, Pallas kernels for 0%

commit v1 on v0

v1 whole, which is shorter than its diff:
```python
import math

import jax
import jax.numpy as jnp
from jax import lax
from jax.experimental import pallas as pl
from jax.experimental.pallas import tpu as pltpu
from jax.sharding import Mesh, PartitionSpec as P

DH = 128
CH = 64
NTOK = 128
NEIGH = 2
BF = jnp.bfloat16
F32 = jnp.float32
DP = ("z", "x", "c")
SPLITS = (112, 112)


def nt(a, b):
    return lax.dot_general(a, b, (((1,), (1,)), ((), ())), preferred_element_type=F32)


def nn(a, b):
    return jnp.dot(a, b, preferred_element_type=F32)


def span_kernel(heads, head_count, quarter, splits, head_ref, *refs):
    n = len(splits)
    pieces = [refs[5 * i : 5 * i + 5] for i in range(n)]
    wt, w, q, g, qt, gt = refs[5 * n : 5 * n + 6]
    slot_out = refs[5 * n + 6 : 6 * n + 6]
    bgt, xt, qg = refs[6 * n + 6 :]
    span = pl.program_id(0)
    half = pl.num_programs(0) // 2
    me = head_ref[0]
    left = lax.rem(me + head_count - 1, head_count)
    right = lax.rem(me + 1, head_count)
    across = lax.rem(me + 2, head_count)

    def put(owner, offset, rows, ref):
        start = pl.multiple_of(owner * quarter + offset, 16)
        for s in range(NEIGH):
            xt[pl.ds(start, rows), s * NTOK : (s + 1) * NTOK] = ref[s]

    offset = 0
    for (own, from_left, from_right, far_low, far_high), rows in zip(pieces, splits):
        put(me, offset, rows, own)
        put(left, offset, rows, from_left)
        put(right, offset, rows, from_right)

        @pl.when(span < half)
        def _(offset=offset, rows=rows, ref=far_low):
            put(across, offset, rows, ref)

        @pl.when(span >= half)
        def _(offset=offset, rows=rows, ref=far_high):
            put(across, offset, rows, ref)

        offset += rows

    kvt = nn(wt[...], xt[...]).astype(BF)
    scale = 1.0 / math.sqrt(DH)
    cols = heads * DH
    for h in range(heads):
        lo, hi = h * DH, (h + 1) * DH
        kt = kvt[lo:hi]
        vt = kvt[cols + lo : cols + hi]
        scores = nn(q[:, lo:hi], kt) * scale
        dprobs = nn(g[:, lo:hi], vt)
        e = jnp.exp(scores - jnp.max(scores, axis=1, keepdims=True))
        probs = e / jnp.sum(e, axis=1, keepdims=True)
        delta = jnp.sum(probs * dprobs, axis=1, keepdims=True)
        ds = (probs * (dprobs - delta) * scale).astype(BF)
        ph = probs.astype(BF)
        bgt[lo:hi, :] = nn(qt[0, lo:hi, :], ds).astype(BF)
        bgt[cols + lo : cols + hi, :] = nn(gt[0, lo:hi, :], ph).astype(BF)
        qg[:, lo:hi] = nt(ds, kt).astype(BF)
    slot = nn(w[...], bgt[...]).astype(BF)
    for j in range(head_count):
        offset = j * quarter
        for out, rows in zip(slot_out, splits):
            for s in range(NEIGH):
                out[j, s] = slot[offset : offset + rows, s * NTOK : (s + 1) * NTOK]
            offset += rows


def span_call(head_id, pieces, wt, w, q, g, qt, gt, head_count):
    splits = [p[0].shape[1] for p in pieces]
    quarter = sum(splits)
    slots = pieces[0][0].shape[0]
    spans = slots // NEIGH
    half = spans // 2
    cols = q.shape[1]
    e = w.shape[0]
    in_specs = []
    for rows in splits:
        block = (NEIGH, rows, NTOK)
        in_specs += [pl.BlockSpec(block, lambda i, h: (i, 0, 0))] * 3
        in_specs.append(pl.BlockSpec(block, lambda i, h: (jnp.minimum(i, half - 1), 0, 0)))
        in_specs.append(pl.BlockSpec(block, lambda i, h: (jnp.maximum(i - half, 0), 0, 0)))
    whole = lambda a: pl.BlockSpec(a.shape, lambda i, h: (0,) * a.ndim)
    row = pl.BlockSpec((CH, cols), lambda i, h: (i, 0))
    turned = pl.BlockSpec((1, cols, CH), lambda i, h: (i, 0, 0))
    in_specs += [whole(wt), whole(w), row, row, turned, turned]
    out_shape = [jax.ShapeDtypeStruct((head_count, slots, rows, NTOK), BF) for rows in splits]
    out_specs = [
        pl.BlockSpec((head_count, NEIGH, rows, NTOK), lambda i, h: (0, i, 0, 0)) for rows in splits
    ]
    keys = NEIGH * NTOK
    for rows in (2 * cols, e):
        out_shape.append(jax.ShapeDtypeStruct((rows, slots * NTOK), BF))
        out_specs.append(pl.BlockSpec((rows, keys), lambda i, h: (0, i)))
    out_shape.append(jax.ShapeDtypeStruct(q.shape, BF))
    out_specs.append(row)

    def body(*refs):
        span_kernel(cols // DH, head_count, quarter, splits, *refs)

    flat = [a for p in pieces for a in p]
    outs = pl.pallas_call(
        body,
        grid_spec=pltpu.PrefetchScalarGridSpec(
            num_scalar_prefetch=1, grid=(spans,), in_specs=in_specs, out_specs=out_specs
        ),
        out_shape=out_shape,
        name="span_grads",
    )(head_id, *flat, wt, w, q, g, qt, gt)
    n = len(splits)
    return outs[:n], outs[n], outs[n + 1], outs[n + 2]


def sum_kernel(idx_ref, valid_ref, r, *rest):
    out, acc = rest[-2], rest[-1]
    acc[...] = jnp.zeros_like(acc)

    def step(o, carry):
        @pl.when(valid_ref[o] > 0)
        def _():
            b = idx_ref[o]
            acc[b] = acc[b] + r[o].astype(F32)

        return carry

    lax.fori_loop(0, r.shape[0], step, 0)
    out[...] = acc[...].astype(BF)


def sum_call(idx, valid, returned, own_blocks, quarter, offset, so_far):
    rows = returned.shape[1]
    step = 16
    base = offset // step
    in_specs = [pl.BlockSpec((returned.shape[0], step, NTOK), lambda i, a, b: (0, i, 0))]
    args = [idx, valid, returned]
    aliases = {}
    if so_far is not None:
        in_specs.append(pl.BlockSpec(memory_space=pl.ANY))
        args.append(so_far)
        aliases = {3: 0}
    return pl.pallas_call(
        sum_kernel,
        grid_spec=pltpu.PrefetchScalarGridSpec(
            num_scalar_prefetch=2,
            grid=(rows // step,),
            in_specs=in_specs,
            out_specs=pl.BlockSpec((own_blocks, step, NTOK), lambda i, a, b: (0, base + i, 0)),
            scratch_shapes=[pltpu.VMEM((own_blocks, step, NTOK), F32)],
        ),
        out_shape=jax.ShapeDtypeStruct((own_blocks, quarter, NTOK), BF),
        input_output_aliases=aliases,
        name="block_sums",
    )(*args)


def rows_at(a, index):
    return a.at[index].get(mode="promise_in_bounds")


def shards(queries, encodings, neighbour_ids, block_place, query_weight, key_weight, value_weight, attn_grad):
    dp_count = lax.axis_size("z") * lax.axis_size("x") * lax.axis_size("c")
    head_count = lax.axis_size("head")
    own_blocks, _, quarter = encodings.shape
    slots = neighbour_ids.size
    cols = key_weight.shape[1]
    head_id = lax.axis_index("head").astype(jnp.int32).reshape(1)

    position = rows_at(block_place, neighbour_ids.reshape(-1))
    owner = position // own_blocks
    local = position % own_blocks
    match = owner[:, None] == jnp.arange(dp_count, dtype=jnp.int32)[None, :]
    requests = jnp.sum(jnp.where(match, local[:, None] + 1, 0), axis=0) - 1
    slot_of = jnp.sum(
        jnp.where(match, jnp.arange(slots, dtype=jnp.int32)[:, None], 0), axis=0
    )
    asked = lax.all_to_all(requests.reshape(dp_count, 1, 1), DP, 0, 0, tiled=True).reshape(-1)
    index = jnp.maximum(asked, 0)
    valid = (asked >= 0).astype(jnp.int32)

    stored = jnp.swapaxes(encodings, 1, 2)
    up = [(i, (i + 1) % head_count) for i in range(head_count)]
    down = [(i, (i - 1) % head_count) for i in range(head_count)]
    pieces = []
    offset = 0
    for rows in SPLITS:
        packed = rows_at(stored[:, offset : offset + rows], index)
        received = lax.all_to_all(packed, DP, 0, 0, tiled=True)
        own = rows_at(received, owner)
        from_left = lax.ppermute(own, "head", up)
        from_right = lax.ppermute(own, "head", down)
        far_low = lax.ppermute(from_left[: slots // 2], "head", up)
        far_high = lax.ppermute(from_right[slots // 2 :], "head", down)
        pieces.append((own, from_left, from_right, far_low, far_high))
        offset += rows

    w = jnp.concatenate([key_weight, value_weight], axis=1)
    spans = slots // NEIGH
    qt = queries.reshape(spans, CH, cols).swapaxes(1, 2)
    gt = attn_grad.reshape(spans, CH, cols).swapaxes(1, 2)
    slot_parts, bgt, xt, query_grad = span_call(
        head_id, pieces, w.T, w, queries, attn_grad, qt, gt, head_count
    )

    encodings_grad = None
    offset = 0
    returned = []
    for part in slot_parts:
        parts = lax.all_to_all(part, "head", 0, 0, tiled=True)
        slot_grad = jnp.sum(parts.astype(F32), axis=0).astype(BF)
        returned.append(lax.all_to_all(rows_at(slot_grad, slot_of), DP, 0, 0, tiled=True))
    for part in returned:
        encodings_grad = sum_call(index, valid, part, own_blocks, quarter, offset, encodings_grad)
        offset += part.shape[1]

    weight_part = nt(xt, bgt)
    e = weight_part.shape[0]
    chips = dp_count // 2
    by_core = weight_part.reshape(chips, 2, e // dp_count, 2 * cols)
    core = lax.axis_index("c")
    mine = lax.dynamic_index_in_dim(by_core, core, 1, keepdims=False)
    other = lax.dynamic_index_in_dim(by_core, 1 - core, 1, keepdims=False)
    pair = mine + lax.ppermute(other, "c", [(0, 1), (1, 0)])
    spread = lax.all_to_all(pair.astype(BF), ("z", "x"), 0, 0, tiled=True)
    weight_grad = jnp.sum(spread.astype(F32), axis=0)

    width = query_weight.shape[0] // head_count
    query_parts = jnp.stack(
        [nt(query_grad, query_weight[j * width : (j + 1) * width]).astype(BF) for j in range(head_count)]
    )
    query_parts = lax.all_to_all(query_parts, "head", 0, 0, tiled=True)
    query_input_grad = jnp.sum(query_parts.astype(F32), axis=0).astype(BF)

    return (
        query_input_grad,
        jnp.swapaxes(encodings_grad, 1, 2),
        weight_grad[:, :cols],
        weight_grad[:, cols:],
    )


def solution(mesh):
    dp, head = mesh.devices.shape
    fine = Mesh(mesh.devices.reshape(dp // 8, 4, 2, head), ("z", "x", "c", "head"))
    in_specs = (
        P(DP, "head"),
        P(DP, None, "head"),
        P(DP, None),
        P(),
        P(None, "head"),
        P(None, "head"),
        P(None, "head"),
        P(DP, "head"),
    )
    out_specs = (P(DP, "head"), P(DP, None, "head"), P(DP, "head"), P(DP, "head"))
    return jax.shard_map(shards, mesh=fine, in_specs=in_specs, out_specs=out_specs, check_vma=False)
```

time: 863 us -> 443 us (0.51)
  waiting for transfers between devices: 594 us -> 209 us
  matrix products: 88.5 us -> 14.7 us
  starting transfers between devices: 22.3 us -> 90.5 us
  local copies, waits for them, and re-layouts: 102 us -> 36.9 us
  Pallas kernels: 0 us -> 53.8 us
  between operations: 14.8 us -> 1 us
    unnamed x5 -> x0, waiting for transfers between devices: 220 us -> none
    all_to_all x2 -> x8, waiting for transfers between devices: 317 us -> 202 us  [the longest x2 81.8 us: shards(): received = lax.all_to_all(packed, DP, 0, 0, tiled=True)]
    dot_general x10 -> x5, matrix products: 88.5 us -> 14.7 us  [nt(): lax.dot_general(a, b, (((1,), (1,)), ((), ())), preferred_element_type=F32)]
    pallas_call x0 -> x3, Pallas kernels: none -> 53.8 us  [the longest x1 35.4 us: span_call(): pl.pallas_call(body, grid_spec=pltpu.PrefetchScalarGridSpec(num_scalar_pr...]
    all_to_all x2 -> x8, starting transfers between devices: 22.1 us -> 71.7 us  [the longest x1 21 us: shards(): spread = lax.all_to_all(pair.astype(BF), ('z', 'x'), 0, 0, tiled=True)]
    reduce_scatter x2 -> x0, waiting for transfers between devices: 32.2 us -> none  [the longest x1 16.9 us: shards(): lax.psum_scatter(partial_input.astype(jnp.bfloat16), 'head', scatter_dime...]
    all_gather x1 -> x0, waiting for transfers between devices: 24.8 us -> none  [shards(): whole_own = lax.all_gather(encodings, 'head', axis=2, tiled=True)]
    ppermute x0 -> x9, starting transfers between devices: none -> 18.7 us  [the longest x1 7.57 us: shards(): pair = mine + lax.ppermute(other, 'c', [(0, 1), (1, 0)])]
  transfers between devices with their start and end apart: 6 -> 17, of which waited for: 5 -> 10; matrix products, arithmetic and copies ran while one was open for 9% -> 12% of each run, Pallas kernels for 0% -> 2%
where the time goes in v1:
time: 443 us; the launch traced here: 441 us
  waiting for transfers between devices  209 us (47%)
  starting transfers between devices  90.5 us (20%)
  Pallas kernels  53.8 us (12%)
  local copies, waits for them, and re-layouts  36.9 us (8%)
  blocking collectives  22.8 us (5%)
  matrix products  14.7 us (3%)
  other arithmetic  13.1 us (3%)
    all_to_all x2, waiting for transfers between devices, shards(): received = lax.all_to_all(packed, DP, 0, 0, tiled=True)  81.8 us
    all_to_all x2, waiting for transfers between devices, shards(): lax.all_to_all(rows_at(slot_grad, slot_of), DP, 0, 0, tiled=True)  72 us
    pallas_call x1, Pallas kernels, span_call(): pl.pallas_call(body, grid_spec=pltpu.PrefetchScalarGridSpec(num_scalar_pr...  35.4 us
    all_to_all x1, blocking collectives, shards(): parts = lax.all_to_all(part, 'head', 0, 0, tiled=True)  22.8 us
    all_to_all x1, starting transfers between devices, shards(): spread = lax.all_to_all(pair.astype(BF), ('z', 'x'), 0, 0, tiled=True)  21 us
    all_to_all x1, waiting for transfers between devices, shards(): spread = lax.all_to_all(pair.astype(BF), ('z', 'x'), 0, 0, tiled=True)  20 us
    pallas_call x2, Pallas kernels, sum_call(): pl.pallas_call(sum_kernel, grid_spec=pltpu.PrefetchScalarGridSpec(num_sca...  18.4 us
    all_to_all x2, starting transfers between devices, shards(): lax.all_to_all(rows_at(slot_grad, slot_of), DP, 0, 0, tiled=True)  17.7 us
  transfers between devices with their start and end apart: 17, of which 10 were waited for; matrix products, arithmetic and copies ran while one was open for 12% of the time, Pallas kernels for 2%

profile of v1, /device:TPU:1, one launch (start us, length us, event | category | flops | bytes accessed | tf_op | source)
XLA Modules:
  0.0 441.4 jit_solution(628962136616856628)
XLA Ops:
  3.0 13.0 %all-to-all-start = ((s32[64,1,1]{2,1,0:T(1,128)}), s32[64,1,1]{2,1,0:T(1,128)S(1)}, u32[]{:S(2)}, u32[]{:S(2)}) async-start(s32[64,1,1]{2,1,0:T(1,128)} %copy.40), calls=%async_computation | async-start | bytes 65536 | tf_op jit(solution)/shard_map/all_to_all | solution.py:195
  17.2 8.1 %all-to-all-done = s32[64,1,1]{2,1,0:T(1,128)S(1)} async-done(((s32[64,1,1]{2,1,0:T(1,128)}), s32[64,1,1]{2,1,0:T(1,128)S(1)}, u32[]{:S(2)}, u32[]{:S(2)}) %all-to-all-start) | async-done | bytes 288 | tf_op jit(solution)/shard_map/all_to_all | solution.py:195
  25.3 2.8 fusion.9
  30.1 4.8 %all-to-all-start.2 = ((bf16[64,112,128]{2,1,0:T(8,128)(2,1)}), bf16[64,112,128]{2,1,0:T(8,128)(2,1)S(1)}, u32[]{:S(2)}, u32[]{:S(2)}) async-start(bf16[64,112,128]{2,1,0:T(8,128)(2,1)} %gather_fusion.3), calls=%async_computation.2 | async-start | bytes 3670016 | tf_op jit(solution)/shard_map/all_to_all | solution.py:206
  37.0 42.5 %all-to-all-done.2 = bf16[64,112,128]{2,1,0:T(8,128)(2,1)S(1)} async-done(((bf16[64,112,128]{2,1,0:T(8,128)(2,1)}), bf16[64,112,128]{2,1,0:T(8,128)(2,1)S(1)}, u32[]{:S(2)}, u32[]{:S(2)}) %all-to-all-start.2) | async-done | bytes 1835040 | tf_op jit(solution)/shard_map/all_to_all | solution.py:206
  80.6 6.7 %all-to-all-start.1 = ((bf16[64,112,128]{2,1,0:T(8,128)(2,1)}), bf16[64,112,128]{2,1,0:T(8,128)(2,1)S(1)}, u32[]{:S(2)}, u32[]{:S(2)}) async-start(bf16[64,112,128]{2,1,0:T(8,128)(2,1)} %gather_fusion.1), calls=%async_computation.1 | async-start | bytes 3670016 | tf_op jit(solution)/shard_map/all_to_all | solution.py:206
  92.4 39.3 %all-to-all-done.1 = bf16[64,112,128]{2,1,0:T(8,128)(2,1)S(1)} async-done(((bf16[64,112,128]{2,1,0:T(8,128)(2,1)}), bf16[64,112,128]{2,1,0:T(8,128)(2,1)S(1)}, u32[]{:S(2)}, u32[]{:S(2)}) %all-to-all-start.1) | async-done | bytes 1835040 | tf_op jit(solution)/shard_map/all_to_all | solution.py:206
  137.8 2.7 collective-permute-start.7
  140.4 3.7 collective-permute-done.refs_2_
  145.8 2.7 collective-permute-start.3
  148.8 2.5 copy.43.refs_11_
  153.9 35.4 %span_grads.1 = (bf16[4,16,112,128]{3,2,1,0:T(8,128)(2,1)}, bf16[4,16,112,128]{3,2,1,0:T(8,128)(2,1)}, bf16[1024,2048]{1,0:T(8,128)(2,1)}, bf16[896,2048]{1,0:T(8,128)(2,1)}, bf16[512,512]{1,0:T(8,128)(2,1)}) custom-call(s32[1]{0:T(128)} %bitcast.refs_0_, bf16[16,112,128]{2,1,0:T(8,128)(2,1)} %copy-done.8, bf16[16,112,128]{2,1,0:T(8,128)(2,1)} %copy-done.10, ...), custom_call_target="tpu_custom_call" | custom-call | tf_op jit(solution)/shard_map/span_grads/pallas_call | solution.py:121
  189.3 22.8 %all_to_all.45 = bf16[4,16,112,128]{3,2,1,0:T(8,128)(2,1)} all-to-all(bf16[4,16,112,128]{3,2,1,0:T(8,128)(2,1)} %get-tuple-element.11), channel_id=1, replica_groups=mesh['z'=8,'x'=4,'c'=2,'head'=4] {'head'}, dimensions={0} | all-to-all | bytes 3670016 | tf_op jit(solution)/shard_map/all_to_all | solution.py:227
  212.1 3.7 all-to-all-start.4
  221.5 2.3 pad_maximum_fusion
  223.8 9.3 %all-to-all-done.4 = bf16[4,16,112,128]{3,2,1,0:T(8,128)(2,1)S(1)} async-done(((bf16[4,16,112,128]{3,2,1,0:T(8,128)(2,1)}), bf16[4,16,112,128]{3,2,1,0:T(8,128)(2,1)S(1)}, u32[]{:S(2)}, u32[]{:S(2)}) %all-to-all-start.4) | async-done | bytes 1835040 | tf_op jit(solution)/shard_map/all_to_all | solution.py:227
  233.0 4.9 %all-to-all-start.3 = ((bf16[4,512,1024]{2,1,0:T(8,128)(2,1)}), bf16[4,512,1024]{2,1,0:T(8,128)(2,1)}, u32[]{:S(2)}, u32[]{:S(2)}) async-start(bf16[4,512,1024]{2,1,0:T(8,128)(2,1)} %pad_maximum_fusion), calls=%async_computation.3 | async-start | bytes 8388608 | tf_op jit(solution)/shard_map/all_to_all | solution.py:249
  237.9 9.1 %fusion.16 = f32[896,1024]{1,0:T(8,128)} fusion(bf16[896,2048]{1,0:T(8,128)(2,1)} %get-tuple-element.12, bf16[1024,2048]{1,0:T(8,128)(2,1)} %get-tuple-element.13), kind=kOutput, calls=%fused_computation.58 | convolution fusion | flops 3758096384 | bytes 11534336 | tf_op jit(solution)/shard_map/dot_general | solution.py:21
  247.0 4.9 %reshape.172 = f32[32,2,14,1024]{3,2,1,0:T(8,128)} reshape(f32[896,1024]{1,0:T(8,128)} %fusion.16) | data formatting | bytes 7340032 | tf_op jit(solution)/shard_map/reshape | solution.py:237
  251.8 2.5 constant_dynamic-slice_fusion.1
  255.5 7.6 %collective-permute-start.8 = (f32[32,14,1024]{2,0,1:T(8,128)S(1)}, f32[32,14,1024]{2,0,1:T(8,128)S(1)}, u32[]{:S(2)}, u32[]{:S(2)}) collective-permute-start(f32[32,14,1024]{2,0,1:T(8,128)S(1)} %bitcast.55), channel_id=1, source_target_pairs={{0,4},{4,0},{1,5},{5,1},{2,6},{6,2},{3,7},{7,3},{8,12},{12,8},{9,1... | collective-permute-start | bytes 5505032 | tf_op jit(solution)/shard_map/ppermute | solution.py:241
  263.0 3.4 collective-permute-done.8
  269.1 10.4 %all-to-all-done.3 = bf16[4,512,1024]{2,1,0:T(8,128)(2,1)} async-done(((bf16[4,512,1024]{2,1,0:T(8,128)(2,1)}), bf16[4,512,1024]{2,1,0:T(8,128)(2,1)}, u32[]{:S(2)}, u32[]{:S(2)}) %all-to-all-start.3) | async-done | bytes 4194336 | tf_op jit(solution)/shard_map/all_to_all | solution.py:249
  279.6 21.0 %all-to-all-start.8 = ((bf16[32,14,1024]{2,1,0:T(8,128)(2,1)}), bf16[32,14,1024]{2,1,0:T(8,128)(2,1)S(1)}, u32[]{:S(2)}, u32[]{:S(2)}) async-start(bf16[32,14,1024]{2,1,0:T(8,128)(2,1)} %copy.46), calls=%async_computation.8 | async-start | bytes 2097152 | tf_op jit(solution)/shard_map/all_to_all | solution.py:242
  304.5 20.0 %all-to-all-done.8 = bf16[32,14,1024]{2,1,0:T(8,128)(2,1)S(1)} async-done(((bf16[32,14,1024]{2,1,0:T(8,128)(2,1)}), bf16[32,14,1024]{2,1,0:T(8,128)(2,1)S(1)}, u32[]{:S(2)}, u32[]{:S(2)}) %all-to-all-start.8) | async-done | bytes 917536 | tf_op jit(solution)/shard_map/all_to_all | solution.py:242
  324.5 11.0 %all-to-all-start.7 = ((bf16[64,112,128]{2,1,0:T(8,128)(2,1)}), bf16[64,112,128]{2,1,0:T(8,128)(2,1)}, u32[]{:S(2)}, u32[]{:S(2)}) async-start(bf16[64,112,128]{2,1,0:T(8,128)(2,1)} %gather_fusion.6), calls=%async_computation.7 | async-start | bytes 3670016 | tf_op jit(solution)/shard_map/all_to_all | solution.py:229
  337.9 42.0 %all-to-all-done.7.r = bf16[64,112,128]{2,1,0:T(8,128)(2,1)} async-done(((bf16[64,112,128]{2,1,0:T(8,128)(2,1)}), bf16[64,112,128]{2,1,0:T(8,128)(2,1)}, u32[]{:S(2)}, u32[]{:S(2)}) %all-to-all-start.7) | async-done | bytes 1835040 | tf_op jit(solution)/shard_map/all_to_all | solution.py:229
  379.9 6.6 %all-to-all-start.5 = ((bf16[64,112,128]{2,1,0:T(8,128)(2,1)}), bf16[64,112,128]{2,1,0:T(8,128)(2,1)S(1)}, u32[]{:S(2)}, u32[]{:S(2)}) async-start(bf16[64,112,128]{2,1,0:T(8,128)(2,1)} %gather_fusion.5), calls=%async_computation.5 | async-start | bytes 3670016 | tf_op jit(solution)/shard_map/all_to_all | solution.py:229
  386.6 4.4 reduce_sum.66
  391.8 9.2 %block_sums.2.rest_0_ = bf16[16,224,128]{2,1,0:T(8,128)(2,1)} custom-call(s32[64]{0:T(128)} %copy-done.14, s32[64]{0:T(128)} %get-tuple-element.14.valid_ref, bf16[64,112,128]{2,1,0:T(8,128)(2,1)} %all-to-all-done.7.r), custom_call_target="tpu_custom_call" | custom-call | tf_op jit(solution)/shard_map/block_sums/pallas_call | solution.py:160
  401.0 30.0 %all-to-all-done.5.r = bf16[64,112,128]{2,1,0:T(8,128)(2,1)S(1)} async-done(((bf16[64,112,128]{2,1,0:T(8,128)(2,1)}), bf16[64,112,128]{2,1,0:T(8,128)(2,1)S(1)}, u32[]{:S(2)}, u32[]{:S(2)}) %all-to-all-start.5) | async-done | bytes 1835040 | tf_op jit(solution)/shard_map/all_to_all | solution.py:229
  432.2 9.1 %block_sums.3 = bf16[16,224,128]{2,1,0:T(8,128)(2,1)} custom-call(s32[64]{0:T(128)} %copy-done.14, s32[64]{0:T(128)} %get-tuple-element.14.valid_ref, bf16[64,112,128]{2,1,0:T(8,128)(2,1)} %copy-done.3, bf16[16,224,128]{2,1,0:T(8,128)(2,1)} %block_sums.2.rest_0_), custom_call_target="tpu_custom_call", output_to_operand_aliasing={{}: (3, {})} | custom-call | tf_op jit(solution)/shard_map/block_sums/pallas_call | solution.py:160
  (87 shorter events, 42.1 us)
Async XLA Ops:
  3.0 22.3 %all-to-all-start = ((s32[64,1,1]{2,1,0:T(1,128)}), s32[64,1,1]{2,1,0:T(1,128)S(1)}, u32[]{:S(2)}, u32[]{:S(2)}) async-start(s32[64,1,1]{2,1,0:T(1,128)} %copy.40), calls=%async_computation | async-start | bytes 65536 | tf_op jit(solution)/shard_map/all_to_all | solution.py:195
  28.1 2.0 copy-start.14
  30.1 49.3 %all-to-all-start.2 = ((bf16[64,112,128]{2,1,0:T(8,128)(2,1)}), bf16[64,112,128]{2,1,0:T(8,128)(2,1)S(1)}, u32[]{:S(2)}, u32[]{:S(2)}) async-start(bf16[64,112,128]{2,1,0:T(8,128)(2,1)} %gather_fusion.3), calls=%async_computation.2 | async-start | bytes 3670016 | tf_op jit(solution)/shard_map/all_to_all | solution.py:206
  79.4 1.2 copy-start.4
  80.6 51.1 %all-to-all-start.1 = ((bf16[64,112,128]{2,1,0:T(8,128)(2,1)}), bf16[64,112,128]{2,1,0:T(8,128)(2,1)S(1)}, u32[]{:S(2)}, u32[]{:S(2)}) async-start(bf16[64,112,128]{2,1,0:T(8,128)(2,1)} %gather_fusion.1), calls=%async_computation.1 | async-start | bytes 3670016 | tf_op jit(solution)/shard_map/all_to_all | solution.py:206
  89.5 59.1 %copy-start.7 = (bf16[16,112,128]{2,1,0:T(8,128)(2,1)}, bf16[16,112,128]{2,1,0:T(8,128)(2,1)S(1)}, u32[]{:S(2)}) copy-start(bf16[16,112,128]{2,1,0:T(8,128)(2,1)S(1)} %gather_fusion.4) | copy-start | bytes 1376260
  89.5 45.8 %collective-permute-start.4 = (bf16[16,112,128]{2,1,0:T(8,128)(2,1)S(1)}, bf16[16,112,128]{2,1,0:T(8,128)(2,1)S(1)}, u32[]{:S(2)}, u32[]{:S(2)}) collective-permute-start(bf16[16,112,128]{2,1,0:T(8,128)(2,1)S(1)} %gather_fusion.4), channel_id=1, source_target_pairs={{0,1},{1,2},{2,3},{3,0},{4,5},{5,6},{6,7},{7,4},{8,9},{9,10},{10,1... | collective-permute-start | bytes 1376264 | tf_op jit(solution)/shard_map/ppermute | solution.py:208
  90.9 45.2 %collective-permute-start.5 = (bf16[16,112,128]{2,1,0:T(8,128)(2,1)S(1)}, bf16[16,112,128]{2,1,0:T(8,128)(2,1)}, u32[]{:S(2)}, u32[]{:S(2)}) collective-permute-start(bf16[16,112,128]{2,1,0:T(8,128)(2,1)S(1)} %gather_fusion.4), channel_id=1, source_target_pairs={{0,3},{1,0},{2,1},{3,2},{4,7},{5,4},{6,5},{7,6},{8,11},{9,8},{10,9... | collective-permute-start | bytes 1376264 | tf_op jit(solution)/shard_map/ppermute | solution.py:209
  132.4 16.4 %copy-start.8 = (bf16[16,112,128]{2,1,0:T(8,128)(2,1)}, bf16[16,112,128]{2,1,0:T(8,128)(2,1)S(1)}, u32[]{:S(2)}) copy-start(bf16[16,112,128]{2,1,0:T(8,128)(2,1)S(1)} %gather_fusion.2) | copy-start | bytes 1376260
  132.4 16.1 %copy-start.12 = (bf16[896,512]{1,0:T(8,128)(2,1)S(1)}, bf16[896,512]{1,0:T(8,128)(2,1)}, u32[]{:S(2)}) copy-start(bf16[896,512]{1,0:T(8,128)(2,1)} %param.13) | copy-start | bytes 2752516
  132.4 16.2 %copy-start.13 = (bf16[896,512]{1,0:T(8,128)(2,1)S(1)}, bf16[896,512]{1,0:T(8,128)(2,1)}, u32[]{:S(2)}) copy-start(bf16[896,512]{1,0:T(8,128)(2,1)} %param.14) | copy-start | bytes 2752516
  132.4 11.7 %collective-permute-start = (bf16[16,112,128]{2,1,0:T(8,128)(2,1)S(1)}, bf16[16,112,128]{2,1,0:T(8,128)(2,1)S(1)}, u32[]{:S(2)}, u32[]{:S(2)}) collective-permute-start(bf16[16,112,128]{2,1,0:T(8,128)(2,1)S(1)} %gather_fusion.2), channel_id=1, source_target_pairs={{0,1},{1,2},{2,3},{3,0},{4,5},{5,6},{6,7},{7,4},{8,9},{9,10},{10,1... | collective-permute-start | bytes 1376264 | tf_op jit(solution)/shard_map/ppermute | solution.py:208
  133.8 11.1 %collective-permute-start.1 = (bf16[16,112,128]{2,1,0:T(8,128)(2,1)S(1)}, bf16[16,112,128]{2,1,0:T(8,128)(2,1)S(1)}, u32[]{:S(2)}, u32[]{:S(2)}) collective-permute-start(bf16[16,112,128]{2,1,0:T(8,128)(2,1)S(1)} %gather_fusion.2), channel_id=1, source_target_pairs={{0,3},{1,0},{2,1},{3,2},{4,7},{5,4},{6,5},{7,6},{8,11},{9,8},{10,9... | collective-permute-start | bytes 1376264 | tf_op jit(solution)/shard_map/ppermute | solution.py:209
  135.3 13.3 %copy-start.9 = (bf16[16,112,128]{2,1,0:T(8,128)(2,1)}, bf16[16,112,128]{2,1,0:T(8,128)(2,1)S(1)}, u32[]{:S(2)}) copy-start(bf16[16,112,128]{2,1,0:T(8,128)(2,1)S(1)} %collective-permute-done.4.refs_7_) | copy-start | bytes 1376260
  136.1 17.8 %collective-permute-start.6 = (bf16[8,112,128]{2,1,0:T(8,128)(2,1)}, bf16[8,112,128]{2,1,0:T(8,128)(2,1)}, u32[]{:S(2)}, u32[]{:S(2)}) collective-permute-start(bf16[8,112,128]{2,1,0:T(8,128)(2,1)} %slice.66), channel_id=1, source_target_pairs={{0,1},{1,2},{2,3},{3,0},{4,5},{5,6},{6,7},{7,4},{8,9},{9,10},{10,1... | collective-permute-start | bytes 688136 | tf_op jit(solution)/shard_map/ppermute | solution.py:210
  137.8 16.2 %collective-permute-start.7 = (bf16[8,112,128]{2,1,0:T(8,128)(2,1)}, bf16[8,112,128]{2,1,0:T(8,128)(2,1)}, u32[]{:S(2)}, u32[]{:S(2)}) collective-permute-start(bf16[8,112,128]{2,1,0:T(8,128)(2,1)} %slice.67), channel_id=1, source_target_pairs={{0,3},{1,0},{2,1},{3,2},{4,7},{5,4},{6,5},{7,6},{8,11},{9,8},{10,9... | collective-permute-start | bytes 688136 | tf_op jit(solution)/shard_map/ppermute | solution.py:211
  144.1 1.5 copy-start.10
  144.9 9.0 %collective-permute-start.2 = (bf16[8,112,128]{2,1,0:T(8,128)(2,1)}, bf16[8,112,128]{2,1,0:T(8,128)(2,1)}, u32[]{:S(2)}, u32[]{:S(2)}) collective-permute-start(bf16[8,112,128]{2,1,0:T(8,128)(2,1)} %slice.63), channel_id=1, source_target_pairs={{0,1},{1,2},{2,3},{3,0},{4,5},{5,6},{6,7},{7,4},{8,9},{9,10},{10,1... | collective-permute-start | bytes 688136 | tf_op jit(solution)/shard_map/ppermute | solution.py:210
  145.8 8.2 %collective-permute-start.3 = (bf16[8,112,128]{2,1,0:T(8,128)(2,1)}, bf16[8,112,128]{2,1,0:T(8,128)(2,1)}, u32[]{:S(2)}, u32[]{:S(2)}) collective-permute-start(bf16[8,112,128]{2,1,0:T(8,128)(2,1)} %slice.64), channel_id=1, source_target_pairs={{0,3},{1,0},{2,1},{3,2},{4,7},{5,4},{6,5},{7,6},{8,11},{9,8},{10,9... | collective-permute-start | bytes 688136 | tf_op jit(solution)/shard_map/ppermute | solution.py:211
  148.7 3.8 copy-start.2
  148.8 2.5 copy-start.6
  148.8 3.8 copy-start.5
  212.1 3.7 copy-start.16
  212.1 20.9 %all-to-all-start.4 = ((bf16[4,16,112,128]{3,2,1,0:T(8,128)(2,1)}), bf16[4,16,112,128]{3,2,1,0:T(8,128)(2,1)S(1)}, u32[]{:S(2)}, u32[]{:S(2)}) async-start(bf16[4,16,112,128]{3,2,1,0:T(8,128)(2,1)} %get-tuple-element.10), calls=%async_computation.4 | async-start | bytes 3670016 | tf_op jit(solution)/shard_map/all_to_all | solution.py:227
  215.9 4.1 copy-start.15
  233.0 46.6 %all-to-all-start.3 = ((bf16[4,512,1024]{2,1,0:T(8,128)(2,1)}), bf16[4,512,1024]{2,1,0:T(8,128)(2,1)}, u32[]{:S(2)}, u32[]{:S(2)}) async-start(bf16[4,512,1024]{2,1,0:T(8,128)(2,1)} %pad_maximum_fusion), calls=%async_computation.3 | async-start | bytes 8388608 | tf_op jit(solution)/shard_map/all_to_all | solution.py:249
  255.5 11.0 %collective-permute-start.8 = (f32[32,14,1024]{2,0,1:T(8,128)S(1)}, f32[32,14,1024]{2,0,1:T(8,128)S(1)}, u32[]{:S(2)}, u32[]{:S(2)}) collective-permute-start(f32[32,14,1024]{2,0,1:T(8,128)S(1)} %bitcast.55), channel_id=1, source_target_pairs={{0,4},{4,0},{1,5},{5,1},{2,6},{6,2},{3,7},{7,3},{8,12},{12,8},{9,1... | collective-permute-start | bytes 5505032 | tf_op jit(solution)/shard_map/ppermute | solution.py:241
  279.6 45.0 %all-to-all-start.8 = ((bf16[32,14,1024]{2,1,0:T(8,128)(2,1)}), bf16[32,14,1024]{2,1,0:T(8,128)(2,1)S(1)}, u32[]{:S(2)}, u32[]{:S(2)}) async-start(bf16[32,14,1024]{2,1,0:T(8,128)(2,1)} %copy.46), calls=%async_computation.8 | async-start | bytes 2097152 | tf_op jit(solution)/shard_map/all_to_all | solution.py:242
  324.5 55.4 %all-to-all-start.7 = ((bf16[64,112,128]{2,1,0:T(8,128)(2,1)}), bf16[64,112,128]{2,1,0:T(8,128)(2,1)}, u32[]{:S(2)}, u32[]{:S(2)}) async-start(bf16[64,112,128]{2,1,0:T(8,128)(2,1)} %gather_fusion.6), calls=%async_computation.7 | async-start | bytes 3670016 | tf_op jit(solution)/shard_map/all_to_all | solution.py:229
  379.9 51.1 %all-to-all-start.5 = ((bf16[64,112,128]{2,1,0:T(8,128)(2,1)}), bf16[64,112,128]{2,1,0:T(8,128)(2,1)S(1)}, u32[]{:S(2)}, u32[]{:S(2)}) async-start(bf16[64,112,128]{2,1,0:T(8,128)(2,1)} %gather_fusion.5), calls=%async_computation.5 | async-start | bytes 3670016 | tf_op jit(solution)/shard_map/all_to_all | solution.py:229
  391.8 49.6 %copy-start.1 = (s32[1024]{0:T(1024)S(1)}, s32[1024]{0:T(1024)}, u32[]{:S(2)}) copy-start(s32[1024]{0:T(1024)} %param.11) | copy-start | bytes 12292
  431.0 1.3 copy-start.3
  (2 other events, 1.7 us)
